TPU v7x, 512 devices: a whole 4x4x16 slice. The times are simulated.
512 devices in a mesh: dp: 16 (over z_lo, core), tensor: 32 (over x, z_hi, y).
Axes of the slice: x: 4, y: 4, z: 16 (z_hi: 2, z_lo: 8; z = z_hi * 8 + z_lo), core: 2. Of those that a mesh axis runs over, the one named last changes fastest.
Arguments:
- activations: bfloat16 [8192, 8192], P('dp', 'tensor'), may hold values from -6 to 6
- left_factor: bfloat16 [1024, 8192], P(None, 'tensor'), may hold values from -0.0625 to 0.0625
- right_factor: bfloat16 [1024, 16384], P(None, 'tensor'), may hold values from -0.1875 to 0.1875
- out_grad: bfloat16 [8192, 16384], P('dp', 'tensor'), may hold values from -6 to 6
Outputs:
- input_grad: bfloat16 [8192, 8192], P('dp', 'tensor')
- left_grad: float32 [1024, 8192], P('dp', 'tensor')
- right_grad: float32 [1024, 16384], P('dp', 'tensor')
All inputs are finite; a program needn't handle non-finite values.
Results may differ from a plain program's by a relative error of at most 0.0049.
Values may be sent and summed in bfloat16 or wider, within the bound.
A program may use at most 64 MiB of HBM per device.

v0:
```python
import math

import jax
import jax.numpy as jnp
from jax import lax
from jax.sharding import Mesh
from jax.sharding import PartitionSpec as P

TENSOR = ("tensor_0", "tensor_1", "tensor_2")


def split_up(x, dim, devices):
    before, after = (x.shape[:dim], x.shape[dim + 1 :])
    return jnp.moveaxis(x.reshape(*before, devices, -1, *after), dim, 0)


def summed_on_arrival(x, axis, dim):
    tiles = split_up(x, dim, lax.axis_size(axis))
    arrived = lax.all_to_all(tiles, axis, split_axis=0, concat_axis=0, tiled=True)
    return arrived.sum(axis=0)


def summed_rows(x, axes, dim):
    far, near = axes
    tiles = split_up(x, dim, lax.axis_size(far))
    nearer = summed_on_arrival(tiles, near, dim + 1)
    arrived = lax.all_to_all(nearer, far, split_axis=0, concat_axis=0, tiled=True)
    return arrived.sum(axis=0)


def rows_for(lines, devices):
    spare = -len(lines) % devices
    return jnp.pad(lines, [(0, spare)] + [(0, 0)] * (lines.ndim - 1))


def from_everyone(x, axis):
    copies = jnp.broadcast_to(x, (lax.axis_size(axis), *x.shape))
    return lax.all_to_all(copies, axis, split_axis=0, concat_axis=0, tiled=True)


def laid_out(tiles, dim):
    lengths = list(tiles.shape[1:])
    lengths[dim] *= tiles.shape[0]
    return jnp.moveaxis(tiles, 0, dim).reshape(lengths)


def gather_axes(x, axes, dim):
    far, near = axes
    first = from_everyone(x, far)
    tiles = jnp.swapaxes(from_everyone(first, near), 0, 1)
    return laid_out(tiles.reshape(-1, *x.shape), dim)


def nested_sum(x, axes):
    lines = x.reshape(-1, x.shape[-1])
    own = summed_rows(rows_for(lines, lax.axis_size(axes[0]) * lax.axis_size(axes[1])), axes, 0)
    whole = gather_axes(own, axes, 0)
    return whole[: len(lines)].reshape(x.shape)


def contract_rows(first, second):
    return lax.dot_general(
        first, second, (((0,), (0,)), ((), ())), preferred_element_type=jnp.float32
    )


def contract_cols(first, second):
    return lax.dot_general(
        first, second, (((1,), (1,)), ((), ())), preferred_element_type=jnp.float32
    )


def shards(activations, left_factor, right_factor, out_grad):
    group_count = lax.axis_size("dp")
    scale = 1.0 / math.sqrt(activations.shape[0] * group_count)
    latent_part = contract_cols(activations, left_factor)
    grad_part = contract_cols(out_grad, right_factor)
    latent = nested_sum(latent_part, (("tensor_0", "tensor_1"), "tensor_2")).astype(jnp.bfloat16)
    columns = latent
    right_sum = summed_on_arrival(contract_rows(columns, out_grad), "dp", 0)
    latent_grad = nested_sum(grad_part, (("tensor_0", "tensor_1"), "tensor_2")).astype(jnp.bfloat16)
    input_grad = jnp.dot(latent_grad, left_factor, preferred_element_type=jnp.float32).astype(
        jnp.bfloat16
    )
    columns = latent_grad
    left_sum = summed_on_arrival(contract_rows(columns, activations), "dp", 0)
    return (input_grad, left_sum * scale, right_sum * scale)


def solution(mesh):
    torus = Mesh(
        mesh.devices.reshape(mesh.shape["dp"], 4, 2, 4), ("dp", "tensor_0", "tensor_1", "tensor_2")
    )
    placed = (P("dp", TENSOR), P(None, TENSOR), P(None, TENSOR), P("dp", TENSOR))
    return jax.shard_map(
        shards,
        mesh=torus,
        in_specs=placed,
        out_specs=(P("dp", TENSOR), P("dp", TENSOR), P("dp", TENSOR)),
        check_vma=False,
    )
```

profile of v0, /device:TPU:97, one launch (start us, length us, event | category | flops | bytes accessed | tf_op | source)
XLA Modules:
  0.0 377.2 jit_solution(12898842169084721)
XLA Ops:
  0.6 0.0 copy-start
  0.6 1.2 copy-done
  1.9 1.8 fusion.4
  3.6 1.5 copy.28
  5.1 0.0 copy-start.4
  5.1 4.3 %all-to-all-start = ((f32[4,8,16,1024]{3,2,1,0:T(8,128)}), f32[4,8,16,1024]{3,2,1,0:T(8,128)S(1)}, u32[]{:S(2)}, u32[]{:S(2)}) async-start(f32[4,8,16,1024]{3,2,1,0:T(8,128)} %bitcast.36), calls=%async_computation | async-start | bytes 4194304 | tf_op jit(solution)/shard_map/all_to_all | solution.py:19
  9.4 0.0 copy-done.4
  9.4 1.5 fusion.5
  10.9 1.4 copy.27
  12.4 22.5 %all-to-all-done = f32[4,8,16,1024]{3,2,1,0:T(8,128)S(1)} async-done(((f32[4,8,16,1024]{3,2,1,0:T(8,128)}), f32[4,8,16,1024]{3,2,1,0:T(8,128)S(1)}, u32[]{:S(2)}, u32[]{:S(2)}) %all-to-all-start) | async-done | bytes 2097184 | tf_op jit(solution)/shard_map/all_to_all | solution.py:19
  34.9 4.4 %all-to-all-start.5 = ((f32[4,8,16,1024]{3,2,1,0:T(8,128)}), f32[4,8,16,1024]{3,2,1,0:T(8,128)}, u32[]{:S(2)}, u32[]{:S(2)}) async-start(f32[4,8,16,1024]{3,2,1,0:T(8,128)} %bitcast.35), calls=%async_computation.5 | async-start | bytes 4194304 | tf_op jit(solution)/shard_map/all_to_all | solution.py:19
  39.3 1.0 reduce_sum.54
  40.3 23.7 %all-to-all-done.5 = f32[4,8,16,1024]{3,2,1,0:T(8,128)} async-done(((f32[4,8,16,1024]{3,2,1,0:T(8,128)}), f32[4,8,16,1024]{3,2,1,0:T(8,128)}, u32[]{:S(2)}, u32[]{:S(2)}) %all-to-all-start.5) | async-done | bytes 2097184 | tf_op jit(solution)/shard_map/all_to_all | solution.py:19
  64.0 14.6 %all-to-all-start.1 = ((f32[8,16,1024]{2,1,0:T(8,128)}), f32[8,16,1024]{2,1,0:T(8,128)S(1)}, u32[]{:S(2)}, u32[]{:S(2)}) async-start(f32[8,16,1024]{2,1,0:T(8,128)} %reduce_sum.54), calls=%async_computation.1 | async-start | bytes 1048576 | tf_op jit(solution)/shard_map/all_to_all | solution.py:27
  78.6 2.6 reduce_sum.57
  81.2 27.9 %all-to-all-done.1 = f32[8,16,1024]{2,1,0:T(8,128)S(1)} async-done(((f32[8,16,1024]{2,1,0:T(8,128)}), f32[8,16,1024]{2,1,0:T(8,128)S(1)}, u32[]{:S(2)}, u32[]{:S(2)}) %all-to-all-start.1) | async-done | bytes 524320 | tf_op jit(solution)/shard_map/all_to_all | solution.py:27
  109.1 3.5 all-to-all-start.6
  112.7 24.3 %all-to-all-done.6 = f32[8,16,1024]{2,1,0:T(8,128)S(1)} async-done(((f32[8,16,1024]{2,1,0:T(8,128)}), f32[8,16,1024]{2,1,0:T(8,128)S(1)}, u32[]{:S(2)}, u32[]{:S(2)}) %all-to-all-start.6) | async-done | bytes 524320 | tf_op jit(solution)/shard_map/all_to_all | solution.py:27
  137.0 0.7 broadcast_in_dim.12
  137.8 5.2 %all-to-all-start.2 = ((bf16[8,16,1024]{2,1,0:T(8,128)(2,1)}), bf16[8,16,1024]{2,1,0:T(8,128)(2,1)S(1)}, u32[]{:S(2)}, u32[]{:S(2)}) async-start(bf16[8,16,1024]{2,1,0:T(8,128)(2,1)} %broadcast_in_dim.12), calls=%async_computation.2 | async-start | bytes 524288 | tf_op jit(solution)/shard_map/all_to_all | solution.py:38
  143.0 14.9 %all-to-all-done.2 = bf16[8,16,1024]{2,1,0:T(8,128)(2,1)S(1)} async-done(((bf16[8,16,1024]{2,1,0:T(8,128)(2,1)}), bf16[8,16,1024]{2,1,0:T(8,128)(2,1)S(1)}, u32[]{:S(2)}, u32[]{:S(2)}) %all-to-all-start.2) | async-done | bytes 262176 | tf_op jit(solution)/shard_map/all_to_all | solution.py:38
  157.9 17.9 %all_to_all.50 = bf16[8,16,1024]{2,1,0:T(8,128)(2,1)S(1)} all-to-all(bf16[8,16,1024]{2,1,0:T(8,128)(2,1)S(1)} %broadcast_in_dim.14), channel_id=1, replica_groups=mesh['dp'=16,'tensor_0'=4,'tensor_1'=2,'tensor_2'=4] {'tensor_0','tensor..., dimensions={0} | all-to-all | bytes 524288 | tf_op jit(solution)/shard_map/all_to_all | solution.py:38
  175.8 0.1 broadcast_in_dim.13
  176.0 15.3 %all_to_all.51 = bf16[4,8,16,1024]{3,2,1,0:T(8,128)(2,1)} all-to-all(bf16[4,8,16,1024]{3,2,1,0:T(8,128)(2,1)S(1)} %broadcast_in_dim.13), channel_id=1, replica_groups=mesh['dp'=16,'tensor_0'=4,'tensor_1'=2,'tensor_2'=4] {'tensor_2'}, dimensions={0} | all-to-all | bytes 2097152 | tf_op jit(solution)/shard_map/all_to_all | solution.py:38
  191.3 1.1 broadcast_in_dim.15
  192.4 3.5 all-to-all-start.8
  195.9 1.3 copy.26
  197.2 0.0 copy-start.1
  197.2 1.3 copy.17
  198.6 2.6 fusion.2
  201.2 0.0 copy-done.1
  201.2 5.7 %all-to-all-done.8 = bf16[4,8,16,1024]{3,2,1,0:T(8,128)(2,1)S(1)} async-done(((bf16[4,8,16,1024]{3,2,1,0:T(8,128)(2,1)}), bf16[4,8,16,1024]{3,2,1,0:T(8,128)(2,1)S(1)}, u32[]{:S(2)}, u32[]{:S(2)}) %all-to-all-start.8) | async-done | bytes 1048608 | tf_op jit(solution)/shard_map/all_to_all | solution.py:38
  206.9 0.0 copy-start.3
  206.9 1.0 copy-done.3
  207.9 18.6 %all-to-all-start.4 = ((f32[16,64,256]{2,1,0:T(8,128)}), f32[16,64,256]{2,1,0:T(8,128)S(1)}, u32[]{:S(2)}, u32[]{:S(2)}) async-start(f32[16,64,256]{2,1,0:T(8,128)} %fusion.2), calls=%async_computation.4 | async-start | bytes 2097152 | tf_op jit(solution)/shard_map/all_to_all | solution.py:19
  226.5 2.3 copy.25
  228.9 1.5 copy.20
  230.4 3.1 fusion
  233.5 41.6 %all-to-all-done.4 = f32[16,64,256]{2,1,0:T(8,128)S(1)} async-done(((f32[16,64,256]{2,1,0:T(8,128)}), f32[16,64,256]{2,1,0:T(8,128)S(1)}, u32[]{:S(2)}, u32[]{:S(2)}) %all-to-all-start.4) | async-done | bytes 1048608 | tf_op jit(solution)/shard_map/all_to_all | solution.py:19
  275.1 0.0 copy-start.2
  275.1 1.0 copy-done.2
  276.0 6.8 %all-to-all-start.9 = ((f32[16,64,512]{2,1,0:T(8,128)}), f32[16,64,512]{2,1,0:T(8,128)S(1)}, u32[]{:S(2)}, u32[]{:S(2)}) async-start(f32[16,64,512]{2,1,0:T(8,128)} %fusion), calls=%async_computation.9 | async-start | bytes 4194304 | tf_op jit(solution)/shard_map/all_to_all | solution.py:19
  282.8 2.5 convolution_convert_fusion
  285.3 1.3 reduce_sum.56
  286.6 0.6 broadcast_multiply_fusion.1
  287.2 89.1 %all-to-all-done.9 = f32[16,64,512]{2,1,0:T(8,128)S(1)} async-done(((f32[16,64,512]{2,1,0:T(8,128)}), f32[16,64,512]{2,1,0:T(8,128)S(1)}, u32[]{:S(2)}, u32[]{:S(2)}) %all-to-all-start.9) | async-done | bytes 2097184 | tf_op jit(solution)/shard_map/all_to_all | solution.py:19
  376.4 0.2 reduce_sum.59
  376.5 0.7 broadcast_multiply_fusion
  (3 shorter events, 0.1 us)
Async XLA Ops:
  0.6 1.2 copy-start
  5.1 4.3 %copy-start.4 = (bf16[512,256]{1,0:T(8,128)(2,1)S(1)}, bf16[512,256]{1,0:T(8,128)(2,1)}, u32[]{:S(2)}) copy-start(bf16[512,256]{1,0:T(8,128)(2,1)} %param.4) | copy-start | bytes 786436
  5.1 29.8 %all-to-all-start = ((f32[4,8,16,1024]{3,2,1,0:T(8,128)}), f32[4,8,16,1024]{3,2,1,0:T(8,128)S(1)}, u32[]{:S(2)}, u32[]{:S(2)}) async-start(f32[4,8,16,1024]{3,2,1,0:T(8,128)} %bitcast.36), calls=%async_computation | async-start | bytes 4194304 | tf_op jit(solution)/shard_map/all_to_all | solution.py:19
  34.9 29.1 %all-to-all-start.5 = ((f32[4,8,16,1024]{3,2,1,0:T(8,128)}), f32[4,8,16,1024]{3,2,1,0:T(8,128)}, u32[]{:S(2)}, u32[]{:S(2)}) async-start(f32[4,8,16,1024]{3,2,1,0:T(8,128)} %bitcast.35), calls=%async_computation.5 | async-start | bytes 4194304 | tf_op jit(solution)/shard_map/all_to_all | solution.py:19
  64.0 45.1 %all-to-all-start.1 = ((f32[8,16,1024]{2,1,0:T(8,128)}), f32[8,16,1024]{2,1,0:T(8,128)S(1)}, u32[]{:S(2)}, u32[]{:S(2)}) async-start(f32[8,16,1024]{2,1,0:T(8,128)} %reduce_sum.54), calls=%async_computation.1 | async-start | bytes 1048576 | tf_op jit(solution)/shard_map/all_to_all | solution.py:27
  109.1 27.9 %all-to-all-start.6 = ((f32[8,16,1024]{2,1,0:T(8,128)}), f32[8,16,1024]{2,1,0:T(8,128)S(1)}, u32[]{:S(2)}, u32[]{:S(2)}) async-start(f32[8,16,1024]{2,1,0:T(8,128)} %reduce_sum.57), calls=%async_computation.6 | async-start | bytes 1048576 | tf_op jit(solution)/shard_map/all_to_all | solution.py:27
  137.8 20.1 %all-to-all-start.2 = ((bf16[8,16,1024]{2,1,0:T(8,128)(2,1)}), bf16[8,16,1024]{2,1,0:T(8,128)(2,1)S(1)}, u32[]{:S(2)}, u32[]{:S(2)}) async-start(bf16[8,16,1024]{2,1,0:T(8,128)(2,1)} %broadcast_in_dim.12), calls=%async_computation.2 | async-start | bytes 524288 | tf_op jit(solution)/shard_map/all_to_all | solution.py:38
  192.4 14.5 %all-to-all-start.8 = ((bf16[4,8,16,1024]{3,2,1,0:T(8,128)(2,1)}), bf16[4,8,16,1024]{3,2,1,0:T(8,128)(2,1)S(1)}, u32[]{:S(2)}, u32[]{:S(2)}) async-start(bf16[4,8,16,1024]{3,2,1,0:T(8,128)(2,1)} %broadcast_in_dim.15), calls=%async_computation.8 | async-start | bytes 2097152 | tf_op jit(solution)/shard_map/all_to_all | solution.py:38
  197.2 4.0 %copy-start.1 = (bf16[4,8,16,1024]{3,2,0,1:T(8,128)(2,1)}, bf16[4,8,16,1024]{3,2,0,1:T(8,128)(2,1)S(1)}, u32[]{:S(2)}) copy-start(bf16[4,8,16,1024]{3,2,0,1:T(8,128)(2,1)S(1)} %copy.26) | copy-start | bytes 3145732
  206.9 1.0 copy-start.3
  207.9 67.1 %all-to-all-start.4 = ((f32[16,64,256]{2,1,0:T(8,128)}), f32[16,64,256]{2,1,0:T(8,128)S(1)}, u32[]{:S(2)}, u32[]{:S(2)}) async-start(f32[16,64,256]{2,1,0:T(8,128)} %fusion.2), calls=%async_computation.4 | async-start | bytes 2097152 | tf_op jit(solution)/shard_map/all_to_all | solution.py:19
  275.1 1.0 copy-start.2
  276.0 100.3 %all-to-all-start.9 = ((f32[16,64,512]{2,1,0:T(8,128)}), f32[16,64,512]{2,1,0:T(8,128)S(1)}, u32[]{:S(2)}, u32[]{:S(2)}) async-start(f32[16,64,512]{2,1,0:T(8,128)} %fusion), calls=%async_computation.9 | async-start | bytes 4194304 | tf_op jit(solution)/shard_map/all_to_all | solution.py:19
where the time goes:
time: 378 us; the launch traced here: 377 us
  waiting for transfers between devices  250 us (66%)
  starting transfers between devices  60.9 us (16%)
  blocking collectives  33.3 us (9%)
  local copies, waits for them, and re-layouts  14.5 us (4%)
  matrix products  11.5 us (3%)
  other arithmetic  6.41 us (2%)
    all_to_all x4, waiting for transfers between devices, summed_on_arrival(): lax.all_to_all(tiles, axis, split_axis=0, concat_axis=0, tiled=True)  177 us
    all_to_all x2, waiting for transfers between devices, summed_rows(): lax.all_to_all(nearer, far, split_axis=0, concat_axis=0, tiled=True)  52.3 us
    all_to_all x4, starting transfers between devices, summed_on_arrival(): lax.all_to_all(tiles, axis, split_axis=0, concat_axis=0, tiled=True)  34.1 us
    all_to_all x2, blocking collectives, from_everyone(): return lax.all_to_all(copies, axis, split_axis=0, concat_axis=0, tiled=True)  33.3 us
    all_to_all x2, waiting for transfers between devices, from_everyone(): return lax.all_to_all(copies, axis, split_axis=0, concat_axis=0, tiled=True)  20.6 us
    all_to_all x2, starting transfers between devices, summed_rows(): lax.all_to_all(nearer, far, split_axis=0, concat_axis=0, tiled=True)  18.1 us
    all_to_all x2, starting transfers between devices, from_everyone(): return lax.all_to_all(copies, axis, split_axis=0, concat_axis=0, tiled=True)  8.68 us
  transfers between devices with their start and end apart: 8, of which 8 were waited for; matrix products, arithmetic and copies ran while one was open for 6% of the time, Pallas kernels for 0%

commit v1 on v0

v1 whole, which is shorter than its diff:
```python
import functools
import math

import jax
import jax.numpy as jnp
from jax import lax
from jax.experimental import pallas as pl
from jax.experimental.pallas import tpu as pltpu
from jax.sharding import PartitionSpec as P

MESH = pl.DeviceIdType.MESH
F32, BF16 = jnp.float32, jnp.bfloat16
NT = (((1,), (1,)), ((), ()))
TN = (((0,), (0,)), ((), ()))


def place(x, y, z, core):
    x, y, z, core = x % 4, y % 4, z % 16, core % 2
    return ((z % 8) * 2 + core, x * 8 + (z // 8) * 4 + y)


def kernel(
    scale,
    act_hbm, left_hbm, right_hbm, cot_hbm,
    ig_ref, lg_ref, rg_ref,
    act, left, right, cot,
    own1, snd1, rcv1, acc2, snd2, rcv2, acc3, snd3, rcv3, lat,
    cs_r, cr_r, cs_l, cr_l, ps_r, pr_r, ps_l, pr_l, ds_r, dr_r, ds_l, dr_l, sum_r, sum_l, fin_r, fin_l,
    in_sem, s1, r1, s2, r2, s3, r3, s4, r4, s5, r5, sc, rc, sp, rp, sd, rd,
):
    d, t = lax.axis_index("dp"), lax.axis_index("tensor")
    x, y, core = t // 8, t % 4, d % 2
    zl = d // 2
    z = ((t // 4) % 2) * 8 + zl
    parity, mine = zl % 2, zl // 2

    def coords(h):
        return (x, y) if h == 0 else (y, x)

    def along(h, da, db):
        return place(x + da, y + db, z, core) if h == 0 else place(x + db, y + da, z, core)

    def remote(src, dst, ssem, rsem, device):
        return pltpu.make_async_remote_copy(
            src_ref=src, dst_ref=dst, send_sem=ssem, recv_sem=rsem,
            device_id=device, device_id_type=MESH,
        )

    loads = [
        pltpu.make_async_copy(src, dst, in_sem.at[i])
        for i, (src, dst) in enumerate(
            ((left_hbm, left), (act_hbm, act), (right_hbm, right), (cot_hbm, cot))
        )
    ]
    for load in loads:
        load.start()

    barrier = pltpu.get_barrier_semaphore()
    peers = [place(x, y, z + 8, core)]
    peers += [place(x, y, (z // 8) * 8 + ((mine + k) % 4) * 2 + parity, core) for k in (2, 1, 3)]
    peers += [place(x, y, (z // 8) * 8 + mine * 2 + 1 - parity, core)]
    peers += [place(x + k, y, z, core) for k in (2, 1, 3)] + [place(x, y + k, z, core) for k in (2, 1, 3)]
    peers += [place(x, y, z, core + 1)]
    for peer in peers:
        pl.semaphore_signal(barrier, inc=1, device_id=peer, device_id_type=MESH)

    def copy1(k, step):
        a, _ = coords(k % 2)
        return remote(
            snd1.at[k, step - 1], rcv1.at[k, step - 1], s1.at[k, step - 1], r1.at[k, step - 1],
            along(k % 2, step, 0),
        )

    def partial_tile(k, step, weights, feats):
        h = k % 2
        a, _ = coords(h)
        row = pl.multiple_of(h * 512 + ((a + step) % 4) * 128, 128)
        tile = lax.dot_general(weights[pl.ds(row, 128), :], feats[...], NT, preferred_element_type=F32)
        tile = tile.reshape(4, 32, 512)
        if step:
            snd1[k, step - 1] = tile.astype(BF16)
        else:
            own1[k] = tile

    order = [(h, step) for step in (2, 1, 3) for h in (0, 1)]
    loads[0].wait()
    loads[1].wait()
    waiting = None
    for n, (h, step) in enumerate(order):
        partial_tile(h, step, left, act)
        if n == 0:
            pl.semaphore_wait(barrier, len(peers))
        if waiting:
            copy1(*waiting).start()
        waiting = (h, step)
    partial_tile(0, 0, left, act)
    copy1(*waiting).start()
    partial_tile(1, 0, left, act)
    loads[2].wait()
    loads[3].wait()
    waiting = None
    for h, step in order:
        partial_tile(2 + h, step, right, cot)
        if waiting:
            copy1(*waiting).start()
        waiting = (2 + h, step)
    partial_tile(2, 0, right, cot)
    copy1(*waiting).start()
    partial_tile(3, 0, right, cot)

    def copy2(k, step):
        _, b = coords(k % 2)
        return remote(
            snd2.at[k, (b + step) % 4], rcv2.at[k, step - 1], s2.at[k, step - 1], r2.at[k, step - 1],
            along(k % 2, 0, step),
        )

    def second(k):
        for step in (1, 3, 2):
            copy1(k, step).wait_recv()
        total = own1[k] + rcv1[k, 0].astype(F32) + rcv1[k, 1].astype(F32) + rcv1[k, 2].astype(F32)
        acc2[k] = total
        snd2[k] = total.astype(BF16)
        for step in (2, 1, 3):
            copy2(k, step).start()

    def copy3(k):
        return remote(snd3.at[k], rcv3.at[k], s3.at[k], r3.at[k], place(x, y, z + 8, core))

    def third(k):
        _, b = coords(k % 2)
        for step in (1, 3, 2):
            copy2(k, step).wait_recv()
        total = acc2[k, b] + rcv2[k, 0].astype(F32) + rcv2[k, 1].astype(F32) + rcv2[k, 2].astype(F32)
        acc3[k] = total
        snd3[k] = total.astype(BF16)
        copy3(k).start()

    def copy4(k, step, arriving=False):
        a, b = coords(k % 2)
        block = lat.at[k, a, (b - step) % 4] if arriving else lat.at[k, a, b]
        return remote(block, block, s4.at[k, step - 1], r4.at[k, step - 1], along(k % 2, 0, step))

    def copy5(k, back, step, arriving=False):
        a, b = coords(k % 2)
        block = lat.at[k, (a - step) % 4 if arriving else a, (b - back) % 4]
        return remote(
            block, block, s5.at[k, back, step - 1], r5.at[k, back, step - 1], along(k % 2, step, 0)
        )

    def fourth(k):
        a, b = coords(k % 2)
        copy3(k).wait_recv()
        lat[k, a, b] = (acc3[k] + rcv3[k].astype(F32)).astype(BF16)
        for step in (2, 1, 3):
            copy4(k, step).start()
        for step in (2, 1, 3):
            copy5(k, 0, step).start()

    def fifth(k):
        for back in (1, 3, 2):
            copy4(k, back, True).wait_recv()
            for step in (2, 1, 3):
                copy5(k, back, step).start()

    def gathered(k):
        for back in (0, 1, 3, 2):
            for step in (1, 3, 2):
                copy5(k, back, step, True).wait_recv()

    for k in range(4):
        second(k)
    for k in range(4):
        third(k)
    for k in range(4):
        fourth(k)
        if k >= 2:
            fifth(k - 2)
    for k in (2, 3):
        fifth(k)

    def sets(k):
        if k < 2:
            return cot, cs_r, cr_r, ps_r, pr_r, sum_r
        return act, cs_l, cr_l, ps_l, pr_l, sum_l

    def core_copy(k):
        _, cs, cr, _, _, _ = sets(k)
        return remote(cs.at[k % 2], cr.at[k % 2], sc.at[k], rc.at[k], place(x, y, z, core + 1))

    def products(k):
        feats, cs, _, _, _, total = sets(k)
        width = feats.shape[1]
        theirs = lat[k, :, pl.ds(2 - 2 * core, 2)].reshape(256, 512)
        cs[k % 2] = jnp.dot(theirs, feats[...], preferred_element_type=F32).reshape(4, 64, width).astype(BF16)
        ours = lat[k, :, pl.ds(2 * core, 2)].reshape(256, 512)
        result = jnp.dot(ours, feats[...], preferred_element_type=F32).reshape(4, 64, width)
        core_copy(k).start()
        total[k % 2] = result

    def pair_copy(k):
        _, _, _, ps, pr, _ = sets(k)
        return remote(
            ps.at[k % 2], pr.at[k % 2], sp.at[k], rp.at[k],
            place(x, y, (z // 8) * 8 + mine * 2 + 1 - parity, core),
        )

    def paired(k):
        _, _, cr, ps, _, total = sets(k)
        core_copy(k).wait_recv()
        for j in range(2):
            other = 2 * j + 1 - parity
            ps[k % 2, j] = (total[k % 2, other] + cr[k % 2, other].astype(F32)).astype(BF16)
        pair_copy(k).start()

    def direct_copy(kind, m):
        ds, dr = (ds_r, dr_r) if kind == 0 else (ds_l, dr_l)
        slot = (m - mine + 3) % 4
        return remote(
            ds.at[m], dr.at[slot], sd.at[kind, m], rd.at[kind, slot],
            place(x, y, (z // 8) * 8 + m * 2 + parity, core),
        )

    def direct(k):
        _, _, cr, _, pr, total = sets(k)
        kind = k // 2
        ds, fin = (ds_r, fin_r) if kind == 0 else (ds_l, fin_l)
        pair_copy(k).wait_recv()
        for j in range(2):
            m = (k % 2) * 2 + j
            ours = 2 * j + parity
            value = total[k % 2, ours] + cr[k % 2, ours].astype(F32) + pr[k % 2, j].astype(F32)

            @pl.when(m != mine)
            def _():
                ds[m] = value.astype(BF16)
                direct_copy(kind, m).start()

            @pl.when(m == mine)
            def _():
                fin[...] = value

    def arrived(kind):
        dr, fin, out = (dr_r, fin_r, rg_ref) if kind == 0 else (dr_l, fin_l, lg_ref)
        total = fin[...]
        for slot in (0, 2, 1):
            remote(
                dr.at[slot], dr.at[slot], sd.at[kind, slot], rd.at[kind, slot], place(x, y, z + 8, core)
            ).wait_recv()
            total = total + dr[slot].astype(F32)
        out[...] = total * scale

    for k in (0, 1):
        gathered(k)
        products(k)
    for k in (0, 1):
        paired(k)
    for k in (0, 1):
        direct(k)
    for k in (2, 3):
        gathered(k)
        products(k)
    for k in (2, 3):
        paired(k)
    for k in (2, 3):
        direct(k)

    for n in range(2):
        rows = pl.ds(n * 256, 256)
        total = lax.dot_general(
            lat[2, :, :, :, rows].reshape(512, 256), left[0:512, :], TN, preferred_element_type=F32
        )
        total += lax.dot_general(
            lat[3, :, :, :, rows].reshape(512, 256), left[512:1024, :], TN, preferred_element_type=F32
        )
        ig_ref[rows, :] = total.astype(BF16)

    arrived(0)
    arrived(1)

    for k in range(4):
        for step in (1, 2, 3):
            copy1(k, step).wait_send()
            copy2(k, step).wait_send()
            copy4(k, step).wait_send()
            for back in range(4):
                copy5(k, back, step).wait_send()
        copy3(k).wait_send()
        core_copy(k).wait_send()
        pair_copy(k).wait_send()
    for kind in range(2):
        for m in range(4):
            @pl.when(m != mine)
            def _():
                direct_copy(kind, m).wait_send()


def shards(activations, left_factor, right_factor, out_grad):
    scale = 1.0 / math.sqrt(activations.shape[0] * lax.axis_size("dp"))
    hbm = pl.BlockSpec(memory_space=pl.ANY)
    vmem = pl.BlockSpec(memory_space=pltpu.VMEM)
    dma = pltpu.SemaphoreType.DMA
    return pl.pallas_call(
        functools.partial(kernel, scale),
        name="lowrank_backward",
        out_shape=(
            jax.ShapeDtypeStruct((512, 256), BF16),
            jax.ShapeDtypeStruct((64, 256), F32),
            jax.ShapeDtypeStruct((64, 512), F32),
        ),
        in_specs=[hbm] * 4,
        out_specs=(vmem,) * 3,
        scratch_shapes=[
            pltpu.VMEM((512, 256), BF16),
            pltpu.VMEM((1024, 256), BF16),
            pltpu.VMEM((1024, 512), BF16),
            pltpu.VMEM((512, 512), BF16),
            pltpu.VMEM((4, 4, 32, 512), F32),
            pltpu.VMEM((4, 3, 4, 32, 512), BF16),
            pltpu.VMEM((4, 3, 4, 32, 512), BF16),
            pltpu.VMEM((4, 4, 32, 512), F32),
            pltpu.VMEM((4, 4, 32, 512), BF16),
            pltpu.VMEM((4, 3, 32, 512), BF16),
            pltpu.VMEM((4, 32, 512), F32),
            pltpu.VMEM((4, 32, 512), BF16),
            pltpu.VMEM((4, 32, 512), BF16),
            pltpu.VMEM((4, 4, 4, 32, 512), BF16),
            pltpu.VMEM((2, 4, 64, 512), BF16),
            pltpu.VMEM((2, 4, 64, 512), BF16),
            pltpu.VMEM((2, 4, 64, 256), BF16),
            pltpu.VMEM((2, 4, 64, 256), BF16),
            pltpu.VMEM((2, 2, 64, 512), BF16),
            pltpu.VMEM((2, 2, 64, 512), BF16),
            pltpu.VMEM((2, 2, 64, 256), BF16),
            pltpu.VMEM((2, 2, 64, 256), BF16),
            pltpu.VMEM((4, 64, 512), BF16),
            pltpu.VMEM((3, 64, 512), BF16),
            pltpu.VMEM((4, 64, 256), BF16),
            pltpu.VMEM((3, 64, 256), BF16),
            pltpu.VMEM((2, 4, 64, 512), F32),
            pltpu.VMEM((2, 4, 64, 256), F32),
            pltpu.VMEM((64, 512), F32),
            pltpu.VMEM((64, 256), F32),
            dma((4,)),
            dma((4, 3)), dma((4, 3)),
            dma((4, 3)), dma((4, 3)),
            dma((4,)), dma((4,)),
            dma((4, 3)), dma((4, 3)),
            dma((4, 4, 3)), dma((4, 4, 3)),
            dma((4,)), dma((4,)),
            dma((4,)), dma((4,)),
            dma((2, 4)), dma((2, 3)),
        ],
        compiler_params=pltpu.CompilerParams(
            collective_id=0, has_side_effects=True, vmem_limit_bytes=48 * 1024 * 1024
        ),
    )(activations, left_factor, right_factor, out_grad)


def solution(mesh):
    return jax.shard_map(
        shards,
        mesh=mesh,
        in_specs=(P("dp", "tensor"), P(None, "tensor"), P(None, "tensor"), P("dp", "tensor")),
        out_specs=(P("dp", "tensor"),) * 3,
        check_vma=False,
    )
```

time: 378 us -> 94.2 us (0.25)
  the two profiles are of different devices: /device:TPU:97 before, /device:TPU:8 now
where the time goes in v1:
time: 94.2 us; the launch traced here: 93.9 us
  Pallas kernels  87 us (92%)
  local copies, waits for them, and re-layouts  6.24 us (7%)
    pallas_call x1, Pallas kernels, shards(): pl.pallas_call(functools.partial(kernel, scale), name='lowrank_backward',...  87 us
    unnamed x11, local copies, waits for them, and re-layouts  6.24 us

profile of v1, /device:TPU:8, one launch (start us, length us, event | category | flops | bytes accessed | tf_op | source)
XLA Modules:
  0.0 93.9 jit_solution(16308355755444480655)
XLA Ops:
  0.6 0.0 copy-start
  0.6 1.2 %copy-done = bf16[1024,512]{1,0:T(8,128)(2,1)S(1)} copy-done((bf16[1024,512]{1,0:T(8,128)(2,1)S(1)}, bf16[1024,512]{1,0:T(8,128)(2,1)}, u32[]{:S(2)}) %copy-start) | copy-done | bytes 1048600
  1.9 0.0 copy-start.1
  1.9 1.0 %copy-done.1 = bf16[1024,256]{1,0:T(8,128)(2,1)S(1)} copy-done((bf16[1024,256]{1,0:T(8,128)(2,1)S(1)}, bf16[1024,256]{1,0:T(8,128)(2,1)}, u32[]{:S(2)}) %copy-start.1) | copy-done | bytes 524312
  2.9 0.0 copy-start.2
  2.9 1.0 %copy-done.2 = bf16[512,512]{1,0:T(8,128)(2,1)S(1)} copy-done((bf16[512,512]{1,0:T(8,128)(2,1)S(1)}, bf16[512,512]{1,0:T(8,128)(2,1)}, u32[]{:S(2)}) %copy-start.2) | copy-done | bytes 524312
  3.9 0.0 copy-start.3
  3.9 0.9 %copy-done.3 = bf16[512,256]{1,0:T(8,128)(2,1)S(1)} copy-done((bf16[512,256]{1,0:T(8,128)(2,1)S(1)}, bf16[512,256]{1,0:T(8,128)(2,1)}, u32[]{:S(2)}) %copy-start.3) | copy-done | bytes 262168
  4.9 87.0 %lowrank_backward.1 = (bf16[512,256]{1,0:T(8,128)(2,1)S(1)}, f32[64,256]{1,0:T(8,128)S(1)}, f32[64,512]{1,0:T(8,128)S(1)}) custom-call(bf16[512,256]{1,0:T(8,128)(2,1)S(1)} %copy-done.3, bf16[1024,256]{1,0:T(8,128)(2,1)S(1)} %copy-done.1, bf16[1024,512]{1,0:T(8,128)(2,1)S(1)} %copy-done, bf16[512,512]{1,0:T(8,128)(2,1)S(1)} %copy-done.2), custom_call_target="tpu_custom_call" | custom-call | tf_op jit(solution)/shard_map/lowrank_backward/pallas_call | solution.py:303
  91.9 0.7 copy.10
  92.6 0.6 copy.11
  93.3 0.7 copy.12
Async XLA Ops:
  0.6 1.2 %copy-start = (bf16[1024,512]{1,0:T(8,128)(2,1)S(1)}, bf16[1024,512]{1,0:T(8,128)(2,1)}, u32[]{:S(2)}) copy-start(bf16[1024,512]{1,0:T(8,128)(2,1)} %right_hbm.1) | copy-start | bytes 3145732
  1.9 1.0 %copy-start.1 = (bf16[1024,256]{1,0:T(8,128)(2,1)S(1)}, bf16[1024,256]{1,0:T(8,128)(2,1)}, u32[]{:S(2)}) copy-start(bf16[1024,256]{1,0:T(8,128)(2,1)} %left_hbm.1) | copy-start | bytes 1572868
  2.9 1.0 %copy-start.2 = (bf16[512,512]{1,0:T(8,128)(2,1)S(1)}, bf16[512,512]{1,0:T(8,128)(2,1)}, u32[]{:S(2)}) copy-start(bf16[512,512]{1,0:T(8,128)(2,1)} %cot_hbm.1) | copy-start | bytes 1572868
  3.9 0.9 %copy-start.3 = (bf16[512,256]{1,0:T(8,128)(2,1)S(1)}, bf16[512,256]{1,0:T(8,128)(2,1)}, u32[]{:S(2)}) copy-start(bf16[512,256]{1,0:T(8,128)(2,1)} %act_hbm.1) | copy-start | bytes 786436

commit v2 on v1

v2 whole, which is shorter than its diff:
```python
import functools
import math

import jax
import jax.numpy as jnp
from jax import lax
from jax.experimental import pallas as pl
from jax.experimental.pallas import tpu as pltpu
from jax.sharding import PartitionSpec as P

MESH = pl.DeviceIdType.MESH
F32, BF16 = jnp.float32, jnp.bfloat16
NT = (((1,), (1,)), ((), ()))
TN = (((0,), (0,)), ((), ()))


def place(x, y, z, core):
    x, y, z, core = x % 4, y % 4, z % 16, core % 2
    return ((z % 8) * 2 + core, x * 8 + (z // 8) * 4 + y)


def kernel(
    scale,
    act_hbm, left_hbm, right_hbm, cot_hbm,
    ig_ref, lg_ref, rg_ref,
    act, left, right, cot,
    own1, snd1, rcv1, acc2, snd2, rcv2, acc3, snd3, rcv3, lat,
    latx, qs_r, qr_r, qs_l, qr_l, hs_r, hr_r, hs_l, hr_l, sum_r, sum_l,
    in_sem, s1, r1, s2, r2, s3, r3, s4, r4, s5, r5, sx, rx, sq, rq, sh, rh,
):
    d, t = lax.axis_index("dp"), lax.axis_index("tensor")
    x, y, core = t // 8, t % 4, d % 2
    zl = d // 2
    z = ((t // 4) % 2) * 8 + zl
    quad, pos = zl // 4, zl % 4

    def coords(h):
        return (x, y) if h == 0 else (y, x)

    def along(h, da, db):
        return place(x + da, y + db, z, core) if h == 0 else place(x + db, y + da, z, core)

    def remote(src, dst, ssem, rsem, device):
        return pltpu.make_async_remote_copy(
            src_ref=src, dst_ref=dst, send_sem=ssem, recv_sem=rsem,
            device_id=device, device_id_type=MESH,
        )

    def mate(step):
        return place(x, y, z - pos + (pos + step) % 4, core)

    opposite = place(x, y, z + 4 - 8 * quad, core)

    loads = [
        pltpu.make_async_copy(src, dst, in_sem.at[i])
        for i, (src, dst) in enumerate(
            ((left_hbm, left), (act_hbm, act.at[core]), (right_hbm, right), (cot_hbm, cot.at[core]))
        )
    ]
    for load in loads:
        load.start()

    barrier = pltpu.get_barrier_semaphore()
    peers = [place(x, y, z + 8, core), place(x, y, z + 8, core + 1)]
    peers += [opposite, *(mate(step) for step in (2, 1, 3))]
    peers += [place(x + k, y, z, core) for k in (2, 1, 3)] + [place(x, y + k, z, core) for k in (2, 1, 3)]
    peers += [place(x, y, z, core + 1)]
    for peer in peers:
        pl.semaphore_signal(barrier, inc=1, device_id=peer, device_id_type=MESH)

    def copy1(k, step):
        a, _ = coords(k % 2)
        return remote(
            snd1.at[k, step - 1], rcv1.at[k, step - 1], s1.at[k, step - 1], r1.at[k, step - 1],
            along(k % 2, step, 0),
        )

    def feature_copies():
        return [
            remote(src, dst.at[core], sx.at[i], rx.at[i], place(x, y, z, core + 1))
            for i, (src, dst) in enumerate(((cot_hbm, cot), (act_hbm, act)))
        ]

    def partial_tile(k, step, weights, feats):
        h = k % 2
        a, _ = coords(h)
        row = pl.multiple_of(h * 512 + ((a + step) % 4) * 128, 128)
        tile = lax.dot_general(weights[pl.ds(row, 128), :], feats[core], NT, preferred_element_type=F32)
        for c in range(2):
            rows = tile[c * 64 : c * 64 + 64].reshape(4, 16, 512)
            if step:
                snd1[k, step - 1, :, c] = rows.astype(BF16)
            else:
                own1[k, :, c] = rows

    order = [(h, step) for step in (2, 1, 3) for h in (0, 1)]
    loads[0].wait()
    loads[1].wait()
    waiting = None
    for n, (h, step) in enumerate(order):
        partial_tile(h, step, left, act)
        if n == 0:
            pl.semaphore_wait(barrier, len(peers))
        if waiting:
            copy1(*waiting).start()
        waiting = (h, step)
    partial_tile(0, 0, left, act)
    copy1(*waiting).start()
    for copy in feature_copies():
        copy.start()
    partial_tile(1, 0, left, act)
    loads[2].wait()
    loads[3].wait()
    for n, (h, step) in enumerate(order):
        partial_tile(2 + h, step, right, cot)
    partial_tile(2, 0, right, cot)
    partial_tile(3, 0, right, cot)

    def copy2(k, step):
        _, b = coords(k % 2)
        return remote(
            snd2.at[k, (b + step) % 4], rcv2.at[k, step - 1], s2.at[k, step - 1], r2.at[k, step - 1],
            along(k % 2, 0, step),
        )

    def second(k):
        for step in (1, 3, 2) if k >= 2 else (1, 3):
            copy1(k, step).wait_recv()
        total = own1[k] + rcv1[k, 0].astype(F32) + rcv1[k, 1].astype(F32) + rcv1[k, 2].astype(F32)
        acc2[k] = total
        snd2[k] = total.astype(BF16)
        for step in (2, 1, 3):
            copy2(k, step).start()

    def copy3(k, way):
        source = snd3.at[k, core if way == 0 else 1 - core]
        device = (place(x, y, z + 8, core), place(x, y, z, core + 1), place(x, y, z + 8, core + 1))[way]
        return remote(source, rcv3.at[k, way], s3.at[k, way], r3.at[k, way], device)

    def third(k):
        _, b = coords(k % 2)
        for step in (1, 3, 2):
            copy2(k, step).wait_recv()
        total = acc2[k, b] + rcv2[k, 0].astype(F32) + rcv2[k, 1].astype(F32) + rcv2[k, 2].astype(F32)
        acc3[k] = total
        snd3[k] = total.astype(BF16)
        for way in (0, 2, 1):
            copy3(k, way).start()

    def copy4(k, step, arriving=False):
        a, b = coords(k % 2)
        block = lat.at[k, a, (b - step) % 4] if arriving else lat.at[k, a, b]
        return remote(block, block, s4.at[k, step - 1], r4.at[k, step - 1], along(k % 2, 0, step))

    def copy5(k, back, step, arriving=False):
        a, b = coords(k % 2)
        block = lat.at[k, (a - step) % 4 if arriving else a, (b - back) % 4]
        return remote(
            block, block, s5.at[k, back, step - 1], r5.at[k, back, step - 1], along(k % 2, step, 0)
        )

    def fourth(k):
        a, b = coords(k % 2)
        for way in (1, 0, 2):
            copy3(k, way).wait_recv()
        lat[k, a, b, core] = (acc3[k, core] + rcv3[k, 0].astype(F32)).astype(BF16)
        lat[k, a, b, 1 - core] = (rcv3[k, 1].astype(F32) + rcv3[k, 2].astype(F32)).astype(BF16)
        for step in (2, 1, 3):
            copy4(k, step).start()
        for step in (2, 1, 3):
            copy5(k, 0, step).start()

    def fifth(k):
        for back in (1, 3, 2):
            copy4(k, back, True).wait_recv()
            for step in (2, 1, 3):
                copy5(k, back, step).start()

    def gathered(k):
        for back in (0, 1, 3, 2):
            for step in (1, 3, 2):
                copy5(k, back, step, True).wait_recv()

    for k in (0, 1):
        copy1(k, 2).wait_recv()
        copy1(2 + k, 2).start()
    for k in (0, 1):
        second(k)
    for h, step in order[2:]:
        copy1(2 + h, step).start()
    for k in (0, 1):
        third(k)
    for k in (2, 3):
        second(k)
    for k in (2, 3):
        third(k)
    for k in (0, 1):
        fourth(k)
    for k in (0, 1):
        fifth(k)
    for k in (2, 3):
        fourth(k)

    kinds = (
        (cot, qs_r, qr_r, hs_r, hr_r, sum_r, rg_ref),
        (act, qs_l, qr_l, hs_l, hr_l, sum_l, lg_ref),
    )

    def products(kind, part):
        feats, total = kinds[kind][0], kinds[kind][5]
        k = kind * 2 + (quad if part else 1 - quad)
        result = jnp.dot(lat[k, :, :, 0].reshape(256, 512), feats[0], preferred_element_type=F32)
        result += jnp.dot(lat[k, :, :, 1].reshape(256, 512), feats[1], preferred_element_type=F32)
        total[part] = result.reshape(4, 64, feats.shape[2])

    def swap_copy(h):
        return remote(
            lat.at[2 + h, :, :, 1 - core], latx.at[h], sx.at[2 + h], rx.at[2 + h], place(x, y, z, core + 1)
        )

    def quad_copy(kind, part, step):
        qs, qr = kinds[kind][1:3]
        return remote(
            qs.at[part, step - 1], qr.at[part, step - 1],
            sq.at[kind, part, step - 1], rq.at[kind, part, step - 1], mate(step),
        )

    def quads(kind, part):
        qs, total = kinds[kind][1], kinds[kind][5]
        for step in (2, 1, 3):
            qs[part, step - 1] = total[part, (pos + step) % 4].astype(BF16)
        for step in (2, 1, 3):
            quad_copy(kind, part, step).start()

    def run_sum(kind, part):
        qr = kinds[kind][2]
        total = kinds[kind][5][part, pos]
        for step in (1, 3, 2):
            quad_copy(kind, part, step).wait_recv()
            total = total + qr[part, step - 1].astype(F32)
        return total

    def half_copy(kind):
        hs, hr = kinds[kind][3:5]
        return remote(hs, hr, sh.at[kind], rh.at[kind], opposite)

    def halves(kind):
        hs = kinds[kind][3]
        hs[...] = run_sum(kind, 0).astype(BF16)
        half_copy(kind).start()

    def finish(kind):
        hr, out = kinds[kind][4], kinds[kind][6]
        total = run_sum(kind, 1)
        half_copy(kind).wait_recv()
        out[...] = (total + hr[...].astype(F32)) * scale

    for copy in feature_copies():
        copy.wait_recv()
    gathered(0)
    gathered(1)
    products(0, 0)
    quads(0, 0)
    fifth(2)
    fifth(3)
    products(0, 1)
    gathered(2)
    gathered(3)
    products(1, 0)
    quads(1, 0)
    halves(0)
    quads(0, 1)
    for h in range(2):
        swap_copy(h).start()
    products(1, 1)
    quads(1, 1)

    def ranks(h, c):
        return jnp.concatenate(
            [left[pl.ds(pl.multiple_of(h * 512 + i * 128 + c * 64, 64), 64), :] for i in range(4)], axis=0
        )

    for h in range(2):
        swap_copy(h).wait_recv()
    total = 0.0
    for h in range(2):
        total += lax.dot_general(
            lat[2 + h, :, :, core].reshape(256, 512), ranks(h, core), TN, preferred_element_type=F32
        )
        total += lax.dot_general(
            latx[h].reshape(256, 512), ranks(h, 1 - core), TN, preferred_element_type=F32
        )
    ig_ref[...] = total.astype(BF16)
    halves(1)
    finish(0)
    finish(1)

    for k in range(4):
        for step in (1, 2, 3):
            copy1(k, step).wait_send()
            copy2(k, step).wait_send()
            copy4(k, step).wait_send()
            for back in range(4):
                copy5(k, back, step).wait_send()
        for way in range(3):
            copy3(k, way).wait_send()
    for copy in feature_copies():
        copy.wait_send()
    for kind in range(2):
        swap_copy(kind).wait_send()
        half_copy(kind).wait_send()
        for part in range(2):
            for step in (1, 2, 3):
                quad_copy(kind, part, step).wait_send()


def put_out(a, b, c, a_out, b_out, c_out, sem):
    copies = [
        pltpu.make_async_copy(src, dst, sem.at[i])
        for i, (src, dst) in enumerate(((a, a_out), (b, b_out), (c, c_out)))
    ]
    for copy in copies:
        copy.start()
    for copy in copies:
        copy.wait()


def shards(activations, left_factor, right_factor, out_grad):
    scale = 1.0 / math.sqrt(activations.shape[0] * lax.axis_size("dp"))
    hbm = pl.BlockSpec(memory_space=pltpu.HBM)
    vmem = pl.BlockSpec(memory_space=pltpu.VMEM)
    dma = pltpu.SemaphoreType.DMA
    results = pl.pallas_call(
        functools.partial(kernel, scale),
        name="lowrank_backward",
        out_shape=(
            jax.ShapeDtypeStruct((512, 256), BF16),
            jax.ShapeDtypeStruct((64, 256), F32),
            jax.ShapeDtypeStruct((64, 512), F32),
        ),
        in_specs=[hbm] * 4,
        out_specs=(vmem,) * 3,
        scratch_shapes=[
            pltpu.VMEM((2, 512, 256), BF16),
            pltpu.VMEM((1024, 256), BF16),
            pltpu.VMEM((1024, 512), BF16),
            pltpu.VMEM((2, 512, 512), BF16),
            pltpu.VMEM((4, 4, 2, 16, 512), F32),
            pltpu.VMEM((4, 3, 4, 2, 16, 512), BF16),
            pltpu.VMEM((4, 3, 4, 2, 16, 512), BF16),
            pltpu.VMEM((4, 4, 2, 16, 512), F32),
            pltpu.VMEM((4, 4, 2, 16, 512), BF16),
            pltpu.VMEM((4, 3, 2, 16, 512), BF16),
            pltpu.VMEM((4, 2, 16, 512), F32),
            pltpu.VMEM((4, 2, 16, 512), BF16),
            pltpu.VMEM((4, 3, 16, 512), BF16),
            pltpu.VMEM((4, 4, 4, 2, 16, 512), BF16),
            pltpu.VMEM((2, 4, 4, 16, 512), BF16),
            pltpu.VMEM((2, 3, 64, 512), BF16),
            pltpu.VMEM((2, 3, 64, 512), BF16),
            pltpu.VMEM((2, 3, 64, 256), BF16),
            pltpu.VMEM((2, 3, 64, 256), BF16),
            pltpu.VMEM((64, 512), BF16),
            pltpu.VMEM((64, 512), BF16),
            pltpu.VMEM((64, 256), BF16),
            pltpu.VMEM((64, 256), BF16),
            pltpu.VMEM((2, 4, 64, 512), F32),
            pltpu.VMEM((2, 4, 64, 256), F32),
            dma((4,)),
            dma((4, 3)), dma((4, 3)),
            dma((4, 3)), dma((4, 3)),
            dma((4, 3)), dma((4, 3)),
            dma((4, 3)), dma((4, 3)),
            dma((4, 4, 3)), dma((4, 4, 3)),
            dma((4,)), dma((4,)),
            dma((2, 2, 3)), dma((2, 2, 3)),
            dma((2,)), dma((2,)),
        ],
        compiler_params=pltpu.CompilerParams(
            collective_id=0, has_side_effects=True, vmem_limit_bytes=56_000_000
        ),
    )(activations, left_factor, right_factor, out_grad)
    return pl.pallas_call(
        put_out,
        name="put_out",
        out_shape=tuple(jax.ShapeDtypeStruct(r.shape, r.dtype) for r in results),
        in_specs=[vmem] * 3,
        out_specs=(pl.BlockSpec(memory_space=pltpu.HBM),) * 3,
        scratch_shapes=[dma((3,))],
        compiler_params=pltpu.CompilerParams(vmem_limit_bytes=1024 * 1024),
    )(*results)


def solution(mesh):
    return jax.shard_map(
        shards,
        mesh=mesh,
        in_specs=(P("dp", "tensor"), P(None, "tensor"), P(None, "tensor"), P("dp", "tensor")),
        out_specs=(P("dp", "tensor"),) * 3,
        check_vma=False,
    )
```

time: 94.2 us -> 76.2 us (0.81)
  the two profiles are of different devices: /device:TPU:8 before, /device:TPU:64 now
where the time goes in v2:
time: 76.2 us; the launch traced here: 76.1 us
  Pallas kernels  75.5 us (99%)
    pallas_call x1, Pallas kernels, shards(): pl.pallas_call(functools.partial(kernel, scale), name='lowrank_backward',...  74.7 us

profile of v2, /device:TPU:64, one launch (start us, length us, event | category | flops | bytes accessed | tf_op | source)
XLA Modules:
  0.0 76.1 jit_solution(6077269083328573391)
XLA Ops:
  0.6 74.7 %lowrank_backward.1 = (bf16[512,256]{1,0:T(8,128)(2,1)S(1)}, f32[64,256]{1,0:T(8,128)S(1)}, f32[64,512]{1,0:T(8,128)S(1)}) custom-call(bf16[512,256]{1,0:T(8,128)(2,1)} %act_hbm.1, bf16[1024,256]{1,0:T(8,128)(2,1)} %left_hbm.1, bf16[1024,512]{1,0:T(8,128)(2,1)} %right_hbm.1, bf16[512,512]{1,0:T(8,128)(2,1)} %cot_hbm.1), custom_call_target="tpu_custom_call" | custom-call | tf_op jit(solution)/shard_map/lowrank_backward/pallas_call | solution.py:333
  75.3 0.8 %put_out.1 = (bf16[512,256]{1,0:T(8,128)(2,1)}, f32[64,256]{1,0:T(8,128)}, f32[64,512]{1,0:T(8,128)}) custom-call(bf16[512,256]{1,0:T(8,128)(2,1)S(1)} %get-tuple-element.6.a, f32[64,256]{1,0:T(8,128)S(1)} %get-tuple-element.7.b, f32[64,512]{1,0:T(8,128)S(1)} %get-tuple-element.8.c), custom_call_target="tpu_custom_call" | custom-call | tf_op jit(solution)/shard_map/put_out/pallas_call | solution.py:383

commit v3 on v2

--- a/solution.py
+++ b/solution.py
@@ -12,6 +12,7 @@
 F32, BF16 = jnp.float32, jnp.bfloat16
 NT = (((1,), (1,)), ((), ()))
 TN = (((0,), (0,)), ((), ()))
+HALF = 256
 
 
 def place(x, y, z, core):
@@ -33,6 +34,10 @@
     zl = d // 2
     z = ((t // 4) % 2) * 8 + zl
     quad, pos = zl // 4, zl % 4
+    outer = (pos == 0) | (pos == 3)
+    inner = (pos == 1) | (pos == 2)
+    near = pos + 1 - 2 * (pos % 2)
+    cross, far = 3 - pos, 3 - near
 
     def coords(h):
         return (x, y) if h == 0 else (y, x)
@@ -46,8 +51,8 @@
             device_id=device, device_id_type=MESH,
         )
 
-    def mate(step):
-        return place(x, y, z - pos + (pos + step) % 4, core)
+    def mate(at):
+        return place(x, y, z - pos + at, core)
 
     opposite = place(x, y, z + 4 - 8 * quad, core)
 
@@ -62,7 +67,7 @@
 
     barrier = pltpu.get_barrier_semaphore()
     peers = [place(x, y, z + 8, core), place(x, y, z + 8, core + 1)]
-    peers += [opposite, *(mate(step) for step in (2, 1, 3))]
+    peers += [opposite, *(mate((pos + step) % 4) for step in (2, 1, 3))]
     peers += [place(x + k, y, z, core) for k in (2, 1, 3)] + [place(x, y + k, z, core) for k in (2, 1, 3)]
     peers += [place(x, y, z, core + 1)]
     for peer in peers:
@@ -71,7 +76,7 @@
     def copy1(k, step):
         a, _ = coords(k % 2)
         return remote(
-            snd1.at[k, step - 1], rcv1.at[k, step - 1], s1.at[k, step - 1], r1.at[k, step - 1],
+            snd1.at[k, (a + step) % 4], rcv1.at[k, step - 1], s1.at[k, step - 1], r1.at[k, step - 1],
             along(k % 2, step, 0),
         )
 
@@ -81,40 +86,36 @@
             for i, (src, dst) in enumerate(((cot_hbm, cot), (act_hbm, act)))
         ]
 
-    def partial_tile(k, step, weights, feats):
-        h = k % 2
-        a, _ = coords(h)
-        row = pl.multiple_of(h * 512 + ((a + step) % 4) * 128, 128)
-        tile = lax.dot_general(weights[pl.ds(row, 128), :], feats[core], NT, preferred_element_type=F32)
-        for c in range(2):
-            rows = tile[c * 64 : c * 64 + 64].reshape(4, 16, 512)
-            if step:
-                snd1[k, step - 1, :, c] = rows.astype(BF16)
-            else:
-                own1[k, :, c] = rows
-
-    order = [(h, step) for step in (2, 1, 3) for h in (0, 1)]
+    def tiles(pair, weights, feats):
+        tokens = pl.ds(pair % 2 * HALF, HALF)
+        for h in range(2):
+            k = pair * 2 + h
+            rows = lax.dot_general(
+                weights[h * 512 : h * 512 + 512, :], feats[core, tokens], NT, preferred_element_type=F32
+            ).reshape(4, 2, 4, 16, HALF)
+            for i in range(4):
+                for c in range(2):
+                    own1[k, i, :, c] = rows[i, c]
+                    snd1[k, i, :, c] = rows[i, c].astype(BF16)
+
+    def send1(pair, *steps):
+        for step in steps:
+            for h in range(2):
+                copy1(pair * 2 + h, step).start()
+
     loads[0].wait()
     loads[1].wait()
-    waiting = None
-    for n, (h, step) in enumerate(order):
-        partial_tile(h, step, left, act)
-        if n == 0:
-            pl.semaphore_wait(barrier, len(peers))
-        if waiting:
-            copy1(*waiting).start()
-        waiting = (h, step)
-    partial_tile(0, 0, left, act)
-    copy1(*waiting).start()
+    tiles(0, left, act)
+    pl.semaphore_wait(barrier, len(peers))
+    send1(0, 2, 1, 3)
+    tiles(1, left, act)
+    send1(1, 2)
     for copy in feature_copies():
         copy.start()
-    partial_tile(1, 0, left, act)
     loads[2].wait()
     loads[3].wait()
-    for n, (h, step) in enumerate(order):
-        partial_tile(2 + h, step, right, cot)
-    partial_tile(2, 0, right, cot)
-    partial_tile(3, 0, right, cot)
+    tiles(2, right, cot)
+    tiles(3, right, cot)
 
     def copy2(k, step):
         _, b = coords(k % 2)
@@ -126,7 +127,8 @@
     def second(k):
         for step in (1, 3, 2) if k >= 2 else (1, 3):
             copy1(k, step).wait_recv()
-        total = own1[k] + rcv1[k, 0].astype(F32) + rcv1[k, 1].astype(F32) + rcv1[k, 2].astype(F32)
+        a, _ = coords(k % 2)
+        total = own1[k, a] + rcv1[k, 0].astype(F32) + rcv1[k, 1].astype(F32) + rcv1[k, 2].astype(F32)
         acc2[k] = total
         snd2[k] = total.astype(BF16)
         for step in (2, 1, 3):
@@ -181,25 +183,9 @@
             for step in (1, 3, 2):
                 copy5(k, back, step, True).wait_recv()
 
-    for k in (0, 1):
-        copy1(k, 2).wait_recv()
-        copy1(2 + k, 2).start()
-    for k in (0, 1):
-        second(k)
-    for h, step in order[2:]:
-        copy1(2 + h, step).start()
-    for k in (0, 1):
-        third(k)
-    for k in (2, 3):
-        second(k)
-    for k in (2, 3):
-        third(k)
-    for k in (0, 1):
-        fourth(k)
-    for k in (0, 1):
-        fifth(k)
-    for k in (2, 3):
-        fourth(k)
+    def both(stage, pair):
+        for h in range(2):
+            stage(pair * 2 + h)
 
     kinds = (
         (cot, qs_r, qr_r, hs_r, hr_r, sum_r, rg_ref),
@@ -208,36 +194,99 @@
 
     def products(kind, part):
         feats, total = kinds[kind][0], kinds[kind][5]
-        k = kind * 2 + (quad if part else 1 - quad)
-        result = jnp.dot(lat[k, :, :, 0].reshape(256, 512), feats[0], preferred_element_type=F32)
-        result += jnp.dot(lat[k, :, :, 1].reshape(256, 512), feats[1], preferred_element_type=F32)
+        result = 0.0
+        for u in range(2):
+            k = kind * 4 + u * 2 + (quad if part else 1 - quad)
+            for c in range(2):
+                result += jnp.dot(
+                    lat[k, :, :, c].reshape(256, HALF), feats[c, u * HALF : u * HALF + HALF],
+                    preferred_element_type=F32,
+                )
         total[part] = result.reshape(4, 64, feats.shape[2])
 
-    def swap_copy(h):
-        return remote(
-            lat.at[2 + h, :, :, 1 - core], latx.at[h], sx.at[2 + h], rx.at[2 + h], place(x, y, z, core + 1)
-        )
-
-    def quad_copy(kind, part, step):
-        qs, qr = kinds[kind][1:3]
-        return remote(
-            qs.at[part, step - 1], qr.at[part, step - 1],
-            sq.at[kind, part, step - 1], rq.at[kind, part, step - 1], mate(step),
-        )
-
-    def quads(kind, part):
-        qs, total = kinds[kind][1], kinds[kind][5]
+    def swap_copy(n):
+        return remote(
+            lat.at[4 + n, :, :, 1 - core], latx.at[n], sx.at[2 + n], rx.at[2 + n], place(x, y, z, core + 1)
+        )
+
+    def quad_copy(part, source, slot, at):
+        qs, qr = kinds[0][1:3]
+        return remote(
+            qs.at[part, source], qr.at[part, slot],
+            sq.at[0, part, source], rq.at[0, part, slot], mate(at),
+        )
+
+    def handed(part):
+        return [quad_copy(part, n, n, near) for n in (2, 3)]
+
+    def straight(part):
+        return quad_copy(part, 0, 0, near)
+
+    def passed(part):
+        return [quad_copy(part, 2, 1, cross), quad_copy(part, 3, 1, far)]
+
+    def quads(part):
+        qs, total = kinds[0][1], kinds[0][5]
+        qs[part, 0] = total[part, near].astype(BF16)
+
+        @pl.when(outer)
+        def _():
+            qs[part, 2] = total[part, far].astype(BF16)
+            qs[part, 3] = total[part, cross].astype(BF16)
+            for copy in handed(part):
+                copy.start()
+
+        straight(part).start()
+
+    def relays(part):
+        qs, qr, total = kinds[0][1], kinds[0][2], kinds[0][5]
+
+        @pl.when(inner)
+        def _():
+            for n, (copy, at) in enumerate(zip(handed(part), (cross, far))):
+                copy.wait_recv()
+                qs[part, 2 + n] = (total[part, at] + qr[part, 2 + n].astype(F32)).astype(BF16)
+            for onward in passed(part):
+                onward.start()
+
+    def quad_sends(part):
+        straight(part).wait_send()
+
+        @pl.when(outer)
+        def _():
+            for copy in handed(part):
+                copy.wait_send()
+
+        @pl.when(inner)
+        def _():
+            for copy in passed(part):
+                copy.wait_send()
+
+    def run_sum(part):
+        qr = kinds[0][2]
+        total = kinds[0][5][part, pos]
+        for slot in (0, 1):
+            quad_copy(part, slot, slot, near).wait_recv()
+            total = total + qr[part, slot].astype(F32)
+        return total
+
+    def direct_copy(part, step):
+        return remote(
+            qs_l.at[part, step - 1], qr_l.at[part, step - 1],
+            sq.at[1, part, step - 1], rq.at[1, part, step - 1], mate((pos + step) % 4),
+        )
+
+    def direct(part):
         for step in (2, 1, 3):
-            qs[part, step - 1] = total[part, (pos + step) % 4].astype(BF16)
+            qs_l[part, step - 1] = sum_l[part, (pos + step) % 4].astype(BF16)
         for step in (2, 1, 3):
-            quad_copy(kind, part, step).start()
-
-    def run_sum(kind, part):
-        qr = kinds[kind][2]
-        total = kinds[kind][5][part, pos]
+            direct_copy(part, step).start()
+
+    def direct_sum(part):
+        total = sum_l[part, pos]
         for step in (1, 3, 2):
-            quad_copy(kind, part, step).wait_recv()
-            total = total + qr[part, step - 1].astype(F32)
+            direct_copy(part, step).wait_recv()
+            total = total + qr_l[part, step - 1].astype(F32)
         return total
 
     def half_copy(kind):
@@ -246,56 +295,80 @@
 
     def halves(kind):
         hs = kinds[kind][3]
-        hs[...] = run_sum(kind, 0).astype(BF16)
+        hs[...] = (direct_sum(0) if kind else run_sum(0)).astype(BF16)
         half_copy(kind).start()
 
     def finish(kind):
         hr, out = kinds[kind][4], kinds[kind][6]
-        total = run_sum(kind, 1)
+        total = direct_sum(1) if kind else run_sum(1)
         half_copy(kind).wait_recv()
         out[...] = (total + hr[...].astype(F32)) * scale
 
+    send1(1, 1, 3)
+    for h in range(2):
+        copy1(h, 2).wait_recv()
+    both(second, 0)
+    send1(2, 2)
+    both(second, 1)
+    send1(2, 1, 3)
+    both(third, 0)
+    both(third, 1)
+    send1(3, 2, 1, 3)
+    both(second, 2)
+    both(third, 2)
+    both(second, 3)
+    both(fourth, 0)
+    both(third, 3)
+    both(fourth, 1)
+    both(fifth, 0)
+    both(fifth, 1)
     for copy in feature_copies():
         copy.wait_recv()
-    gathered(0)
-    gathered(1)
+    both(fourth, 2)
+    both(gathered, 0)
+    both(fourth, 3)
+    both(gathered, 1)
     products(0, 0)
-    quads(0, 0)
-    fifth(2)
-    fifth(3)
+    quads(0)
+    both(fifth, 2)
+    both(fifth, 3)
     products(0, 1)
-    gathered(2)
-    gathered(3)
+    quads(1)
+    relays(0)
+    both(gathered, 2)
+    both(gathered, 3)
     products(1, 0)
-    quads(1, 0)
+    direct(0)
+    relays(1)
     halves(0)
-    quads(0, 1)
-    for h in range(2):
-        swap_copy(h).start()
     products(1, 1)
-    quads(1, 1)
+    direct(1)
+    for n in range(4):
+        swap_copy(n).start()
 
     def ranks(h, c):
         return jnp.concatenate(
             [left[pl.ds(pl.multiple_of(h * 512 + i * 128 + c * 64, 64), 64), :] for i in range(4)], axis=0
         )
 
-    for h in range(2):
-        swap_copy(h).wait_recv()
-    total = 0.0
-    for h in range(2):
-        total += lax.dot_general(
-            lat[2 + h, :, :, core].reshape(256, 512), ranks(h, core), TN, preferred_element_type=F32
-        )
-        total += lax.dot_general(
-            latx[h].reshape(256, 512), ranks(h, 1 - core), TN, preferred_element_type=F32
-        )
-    ig_ref[...] = total.astype(BF16)
     halves(1)
+    for n in range(4):
+        swap_copy(n).wait_recv()
+    for u in range(2):
+        total = 0.0
+        for h in range(2):
+            n = u * 2 + h
+            total += lax.dot_general(
+                lat[4 + n, :, :, core].reshape(256, HALF), ranks(h, core), TN, preferred_element_type=F32
+            )
+            total += lax.dot_general(
+                latx[n].reshape(256, HALF), ranks(h, 1 - core), TN, preferred_element_type=F32
+            )
+        ig_ref[u * HALF : u * HALF + HALF, :] = total.astype(BF16)
     finish(0)
     finish(1)
 
-    for k in range(4):
+    for k in range(8):
         for step in (1, 2, 3):
             copy1(k, step).wait_send()
             copy2(k, step).wait_send()
@@ -306,12 +379,14 @@
             copy3(k, way).wait_send()
     for copy in feature_copies():
         copy.wait_send()
+    for n in range(4):
+        swap_copy(n).wait_send()
+    for part in range(2):
+        quad_sends(part)
+        for step in (1, 2, 3):
+            direct_copy(part, step).wait_send()
     for kind in range(2):
-        swap_copy(kind).wait_send()
         half_copy(kind).wait_send()
-        for part in range(2):
-            for step in (1, 2, 3):
-                quad_copy(kind, part, step).wait_send()
 
 
 def put_out(a, b, c, a_out, b_out, c_out, sem):
@@ -345,19 +420,19 @@
             pltpu.VMEM((1024, 256), BF16),
             pltpu.VMEM((1024, 512), BF16),
             pltpu.VMEM((2, 512, 512), BF16),
-            pltpu.VMEM((4, 4, 2, 16, 512), F32),
-            pltpu.VMEM((4, 3, 4, 2, 16, 512), BF16),
-            pltpu.VMEM((4, 3, 4, 2, 16, 512), BF16),
-            pltpu.VMEM((4, 4, 2, 16, 512), F32),
-            pltpu.VMEM((4, 4, 2, 16, 512), BF16),
-            pltpu.VMEM((4, 3, 2, 16, 512), BF16),
-            pltpu.VMEM((4, 2, 16, 512), F32),
-            pltpu.VMEM((4, 2, 16, 512), BF16),
-            pltpu.VMEM((4, 3, 16, 512), BF16),
-            pltpu.VMEM((4, 4, 4, 2, 16, 512), BF16),
-            pltpu.VMEM((2, 4, 4, 16, 512), BF16),
-            pltpu.VMEM((2, 3, 64, 512), BF16),
-            pltpu.VMEM((2, 3, 64, 512), BF16),
+            pltpu.VMEM((8, 4, 4, 2, 16, 256), F32),
+            pltpu.VMEM((8, 4, 4, 2, 16, 256), BF16),
+            pltpu.VMEM((8, 3, 4, 2, 16, 256), BF16),
+            pltpu.VMEM((8, 4, 2, 16, 256), F32),
+            pltpu.VMEM((8, 4, 2, 16, 256), BF16),
+            pltpu.VMEM((8, 3, 2, 16, 256), BF16),
+            pltpu.VMEM((8, 2, 16, 256), F32),
+            pltpu.VMEM((8, 2, 16, 256), BF16),
+            pltpu.VMEM((8, 3, 16, 256), BF16),
+            pltpu.VMEM((8, 4, 4, 2, 16, 256), BF16),
+            pltpu.VMEM((4, 4, 4, 16, 256), BF16),
+            pltpu.VMEM((2, 4, 64, 512), BF16),
+            pltpu.VMEM((2, 4, 64, 512), BF16),
             pltpu.VMEM((2, 3, 64, 256), BF16),
             pltpu.VMEM((2, 3, 64, 256), BF16),
             pltpu.VMEM((64, 512), BF16),
@@ -367,13 +442,13 @@
             pltpu.VMEM((2, 4, 64, 512), F32),
             pltpu.VMEM((2, 4, 64, 256), F32),
             dma((4,)),
-            dma((4, 3)), dma((4, 3)),
-            dma((4, 3)), dma((4, 3)),
-            dma((4, 3)), dma((4, 3)),
-            dma((4, 3)), dma((4, 3)),
-            dma((4, 4, 3)), dma((4, 4, 3)),
-            dma((4,)), dma((4,)),
-            dma((2, 2, 3)), dma((2, 2, 3)),
+            dma((8, 3)), dma((8, 3)),
+            dma((8, 3)), dma((8, 3)),
+            dma((8, 3)), dma((8, 3)),
+            dma((8, 3)), dma((8, 3)),
+            dma((8, 4, 3)), dma((8, 4, 3)),
+            dma((6,)), dma((6,)),
+            dma((2, 2, 4)), dma((2, 2, 4)),
             dma((2,)), dma((2,)),
         ],
         compiler_params=pltpu.CompilerParams(

time: 76.2 us -> 74.2 us (0.974)
  Pallas kernels: 75.5 us -> 73.4 us
    pallas_call x1, Pallas kernels: 74.7 us -> 72.6 us  [shards(): pl.pallas_call(functools.partial(kernel, scale), name='lowrank_backward',...]
where the time goes in v3:
time: 74.2 us; the launch traced here: 74 us
  Pallas kernels  73.4 us (99%)
    pallas_call x1, Pallas kernels, shards(): pl.pallas_call(functools.partial(kernel, scale), name='lowrank_backward',...  72.6 us

profile of v3, /device:TPU:64, one launch (start us, length us, event | category | flops | bytes accessed | tf_op | source)
XLA Modules:
  0.0 74.0 jit_solution(1239959825774736253)
XLA Ops:
  0.6 72.6 %lowrank_backward.1 = (bf16[512,256]{1,0:T(8,128)(2,1)S(1)}, f32[64,256]{1,0:T(8,128)S(1)}, f32[64,512]{1,0:T(8,128)S(1)}) custom-call(bf16[512,256]{1,0:T(8,128)(2,1)} %act_hbm.1, bf16[1024,256]{1,0:T(8,128)(2,1)} %left_hbm.1, bf16[1024,512]{1,0:T(8,128)(2,1)} %right_hbm.1, bf16[512,512]{1,0:T(8,128)(2,1)} %cot_hbm.1), custom_call_target="tpu_custom_call" | custom-call | tf_op jit(solution)/shard_map/lowrank_backward/pallas_call | solution.py:408
  73.2 0.8 %put_out.1 = (bf16[512,256]{1,0:T(8,128)(2,1)}, f32[64,256]{1,0:T(8,128)}, f32[64,512]{1,0:T(8,128)}) custom-call(bf16[512,256]{1,0:T(8,128)(2,1)S(1)} %get-tuple-element.6.a, f32[64,256]{1,0:T(8,128)S(1)} %get-tuple-element.7.b, f32[64,512]{1,0:T(8,128)S(1)} %get-tuple-element.8.c), custom_call_target="tpu_custom_call" | custom-call | tf_op jit(solution)/shard_map/put_out/pallas_call | solution.py:458
